TPU v7x, 256 devices: a whole 4x4x8 slice. The times are simulated.
256 devices in a mesh: term: 4 (over x), sector: 64 (over y, z, core).
Axes of the slice: x: 4, y: 4, z: 8, core: 2. Of those that a mesh axis runs over, the one named last changes fastest.
Arguments:
- psi_blocks: bfloat16 [4096, 128, 128], P('sector'), may hold values from -6 to 6
- right_ops: bfloat16 [8, 4096, 128, 128], P('term', 'sector'), may hold values from -0.5 to 0.5
- left_ops: bfloat16 [8, 4096, 128, 128], P('term', 'sector'), may hold values from -0.1875 to 0.1875
- owner_map: int32 [4096, 1], P('sector'), may hold values from 0 to 63; in each aligned block of 64 rows (0 to 63, 64 to 127, ...) at most 2 rows name the same one
- left_local: int32 [4096, 1], P('sector'), may hold values from 0 to 63
Outputs:
- sigma: bfloat16 [4096, 128, 128], P('sector', 'term')
Inputs may be any that keep to these rules, and one draw needn't show every extreme that they name: `owner_map`: among the 64 sectors held by one device along `sector` (aligned blocks), at most 2 name the same owner; some block reaches it.
All inputs are finite; a program needn't handle non-finite values.
Results may differ from a plain program's by a relative error of at most 0.0049.
Values may be sent and summed in bfloat16 or wider, within the bound.
A program may use at most 128 MiB of HBM per device.

v0:
```python
import jax
import jax.numpy as jnp
from jax import lax
from jax.sharding import PartitionSpec as P


def ranks_of(owners):
    count = owners.shape[-1]
    same = owners[..., :, None] == owners[..., None, :]
    earlier = lax.broadcasted_iota(jnp.int32, (count, count), 0) < lax.broadcasted_iota(
        jnp.int32, (count, count), 1
    )
    return jnp.sum((same & earlier).astype(jnp.int32), axis=-2)


def local(psi_blocks, right_ops, left_ops, owner_map, left_local):
    sec_dev = psi_blocks.shape[0]
    width = psi_blocks.shape[1]
    terms_dev = right_ops.shape[0]
    n_sector = lax.axis_size("sector")
    capacity = max(2, 2 * sec_dev // n_sector)
    slots = n_sector * capacity
    owners = owner_map[:, 0]
    slot_id = owners * capacity + ranks_of(owners)
    packer = (lax.broadcasted_iota(jnp.int32, (slots, sec_dev), 0) == slot_id[None, :]).astype(
        jnp.bfloat16
    )
    routes_all = lax.all_gather(
        jnp.concatenate([owner_map, left_local], axis=1), "sector", axis=0, tiled=True
    )
    all_owners = routes_all[:, 0].reshape(n_sector, sec_dev)
    all_local = routes_all[:, 1].reshape(n_sector, sec_dev)
    all_ranks = ranks_of(all_owners)
    mine = lax.axis_index("sector")
    slot_iota = lax.broadcasted_iota(jnp.int32, (1, 1, capacity), 2)
    hits = (all_owners == mine)[:, :, None] & (all_ranks[:, :, None] == slot_iota)
    tags = (jnp.sum(jnp.where(hits, all_local[:, :, None] + 1, 0), axis=1) - 1).reshape(slots)
    inter = jnp.einsum(
        "sij,tsjk->stik", psi_blocks, right_ops, preferred_element_type=jnp.float32
    ).astype(jnp.bfloat16)
    packed = jnp.dot(packer, inter.reshape(sec_dev, -1), preferred_element_type=jnp.float32).astype(
        jnp.bfloat16
    )
    arrived = lax.all_to_all(
        packed.reshape(n_sector, capacity, -1), "sector", split_axis=0, concat_axis=0, tiled=True
    )
    arrived = arrived.reshape(slots, terms_dev, width, width)
    picked = jnp.take(left_ops, jnp.clip(tags, 0, sec_dev - 1), axis=1)
    images = jnp.einsum("tnij,ntjk->nik", picked, arrived, preferred_element_type=jnp.float32)
    collect = (lax.broadcasted_iota(jnp.int32, (sec_dev, slots), 0) == tags[None, :]).astype(
        jnp.float32
    )
    partial_sum = jnp.dot(
        collect,
        images.reshape(slots, -1),
        precision=lax.Precision.HIGHEST,
        preferred_element_type=jnp.float32,
    ).reshape(sec_dev, width, width)
    total = lax.psum(partial_sum, "term")
    row_count = width // lax.axis_size("term")
    mine_rows = lax.dynamic_slice_in_dim(total, lax.axis_index("term") * row_count, row_count, 1)
    return mine_rows.astype(jnp.bfloat16)


def solution(mesh):
    placed = (
        P("sector", None, None),
        P("term", "sector", None, None),
        P("term", "sector", None, None),
        P("sector", None),
        P("sector", None),
    )
    return jax.shard_map(
        local, mesh=mesh, in_specs=placed, out_specs=P("sector", "term", None), check_vma=False
    )
```

profile of v0, /device:TPU:1, one launch (start us, length us, event | category | flops | bytes accessed | tf_op | source)
XLA Modules:
  0.0 411.3 jit_solution(9655905848802338681)
XLA Ops:
  0.0 0.0 copy-start
  0.0 0.9 convert_reduce_fusion.1
  0.9 0.7 multiply_add_fusion
  1.6 0.0 copy-done
  1.6 5.4 %convert_bitcast_fusion = bf16[64,2,128,128]{2,3,1,0:T(8,128)(2,1)} fusion(bf16[2,64,128,128]{3,2,1,0:T(8,128)(2,1)} %param.6, bf16[64,128,128]{2,1,0:T(8,128)(2,1)S(1)} %copy-done), kind=kOutput, calls=%fused_computation.12 | convolution fusion | flops 538968064 | bytes 10485760 | tf_op jit(solution)/shard_map/sij,tsjk->stik/dot_general | solution.py:38
  7.0 6.3 %copy.23 = bf16[64,2,128,128]{3,2,1,0:T(8,128)(2,1)} copy(bf16[64,2,128,128]{2,3,1,0:T(8,128)(2,1)} %convert_bitcast_fusion) | data formatting | bytes 8388608 | tf_op jit(solution)/shard_map/convert_element_type | solution.py:40
  13.4 8.8 %convolution_convert_fusion = bf16[128,32768]{1,0:T(8,128)(2,1)} fusion(bf16[8,8,256,128]{3,2,1,0:T(8,128)(2,1)} %bitcast.41, s32[64]{0:T(128)S(1)} %multiply_add_fusion), kind=kOutput, calls=%fused_computation.1 | convolution fusion | flops 541073408 | bytes 12583168 | tf_op jit(solution)/shard_map/dot_general | solution.py:41
  22.1 14.1 %reshape.90 = bf16[64,2,32768]{2,1,0:T(2,128)(2,1)} reshape(bf16[128,32768]{1,0:T(8,128)(2,1)} %convolution_convert_fusion) | data formatting | bytes 16777216 | tf_op jit(solution)/shard_map/reshape | solution.py:45
  36.3 13.5 %all-to-all-start = ((bf16[64,2,32768]{2,1,0:T(2,128)(2,1)}), bf16[64,2,32768]{2,1,0:T(2,128)(2,1)}, u32[]{:S(2)}, u32[]{:S(2)}) async-start(bf16[64,2,32768]{2,1,0:T(2,128)(2,1)} %reshape.90), calls=%async_computation | async-start | bytes 16777216 | tf_op jit(solution)/shard_map/all_to_all | solution.py:44
  49.8 0.0 copy-done.2
  49.8 0.0 copy-done.3
  49.8 218.2 %all-gather = s32[64,64,2]{1,2,0:T(2,128)S(1)} all-gather(s32[1,64,2]{1,2,0:T(2,128)S(1)} %add_bitcast_fusion), channel_id=1, replica_groups=mesh['term'=4,'sector'=64] {'sector'}, dimensions={0}, use_global_device_ids=true | all-gather | bytes 33280 | tf_op jit(solution)/shard_map/all_gather | solution.py:28
  268.0 0.1 reshape.102
  268.1 0.1 slice_reduce_fusion
  268.2 0.1 reshape_squeeze.3
  268.3 0.1 add.66
  268.4 0.9 convert_reduce_fusion
  269.3 0.1 select_reduce_fusion
  269.4 0.1 copy.20
  269.5 0.1 sub.7
  269.7 0.1 copy.21
  269.8 0.1 min.18
  269.9 8.6 %gather_fusion = bf16[128,2,128,128]{3,2,1,0:T(8,128)(2,1)} fusion(bf16[2,64,128,128]{3,2,1,0:T(8,128)(2,1)} %param.7, s32[1024]{0:T(1024)S(1)} %pad_clamp_fusion), kind=kCustom, calls=%fused_computation | custom fusion | bytes 16777728 | tf_op jit(solution)/shard_map/jit(_take)/gather | solution.py:48
  278.5 0.0 all-to-all-done
  278.5 14.6 %reshape.91 = bf16[128,2,128,128]{3,2,1,0:T(8,128)(2,1)} reshape(bf16[64,2,32768]{2,1,0:T(2,128)(2,1)} %all-to-all-done) | data formatting | bytes 16777216 | tf_op jit(solution)/shard_map/reshape | solution.py:47
  293.1 8.2 %fusion = f32[128,128,128,1]{2,1,3,0:T(8,128)S(1)} fusion(bf16[128,2,128,128]{3,2,1,0:T(8,128)(2,1)} %reshape.91, bf16[128,2,128,128]{3,2,1,0:T(8,128)(2,1)} %gather_fusion, pred[128]{0:T(512)(128)(4,1)S(1)} %compare_and_fusion), kind=kOutput, calls=%fused_computation.3 | convolution fusion | flops 1077936128 | bytes 25165952 | tf_op jit(solution)/shard_map/tnij,ntjk->nik/dot_general | solution.py:49
  301.3 9.7 %copy.41 = f32[16,8,128,128]{3,1,2,0:T(8,128)} copy(f32[16,8,128,128]{3,2,1,0:T(8,128)S(1)} %bitcast.38) | data formatting | bytes 16777216
  311.1 9.0 %copy.24 = f32[16384,128]{1,0:T(8,128)} copy(f32[16384,128]{0,1:T(8,128)} %bitcast.40) | data formatting | bytes 16777216 | tf_op jit(solution)/shard_map/dot_general | solution.py:53
  320.1 10.5 %fusion.15 = f32[64,128,128]{2,0,1:T(8,128)} fusion(f32[128,128,128]{2,1,0:T(8,128)} %bitcast.39, s32[128]{0:T(128)S(1)} %sub.7), kind=kOutput, calls=%fused_computation.25 | convolution fusion | flops 1610620928 | bytes 12583424 | tf_op jit(solution)/shard_map/dot_general | solution.py:53
  330.6 78.5 %all-reduce.1 = bf16[64,128,128]{2,0,1:T(8,128)(2,1)} all-reduce(f32[64,128,128]{2,0,1:T(8,128)} %fusion.15), channel_id=1, replica_groups=mesh['term'=4,'sector'=64] {'term'}, use_global_device_ids=true, to_apply=%region_3.4 | all-reduce | flops 1048576 | bytes 6291456 | tf_op jit(solution)/shard_map/psum | solution.py:59
  409.1 1.1 dynamic-slice_convert_fusion
  410.2 1.1 copy.25
  (12 shorter events, 0.1 us)
Async XLA Ops:
  0.0 1.6 copy-start
  36.3 13.5 %copy-start.2 = (s32[64,1]{0,1:T(1,128)S(1)}, s32[64,1]{0,1:T(1,128)}, u32[]{:S(2)}) copy-start(s32[64,1]{0,1:T(1,128)} %param.8) | copy-start | bytes 772
  36.3 13.5 %copy-start.3 = (s32[64,1]{0,1:T(1,128)S(1)}, s32[64,1]{0,1:T(1,128)}, u32[]{:S(2)}) copy-start(s32[64,1]{0,1:T(1,128)} %param.9) | copy-start | bytes 772
  36.3 242.2 %all-to-all-start = ((bf16[64,2,32768]{2,1,0:T(2,128)(2,1)}), bf16[64,2,32768]{2,1,0:T(2,128)(2,1)}, u32[]{:S(2)}, u32[]{:S(2)}) async-start(bf16[64,2,32768]{2,1,0:T(2,128)(2,1)} %reshape.90), calls=%async_computation | async-start | bytes 16777216 | tf_op jit(solution)/shard_map/all_to_all | solution.py:44
  320.1 91.2 %copy-start.1 = (bf16[64,128,128]{2,1,0:T(8,128)(2,1)S(1)}, bf16[64,128,128]{2,1,0:T(8,128)(2,1)}, u32[]{:S(2)}) copy-start(bf16[64,128,128]{2,1,0:T(8,128)(2,1)} %param.5) | copy-start | bytes 6291460
where the time goes:
time: 413 us; the launch traced here: 411 us
  blocking collectives  297 us (72%)
  local copies, waits for them, and re-layouts  65.4 us (16%)
  matrix products  32.9 us (8%)
  starting transfers between devices  13.5 us (3%)
    all_gather x1, blocking collectives, local(): lax.all_gather(jnp.concatenate([owner_map, left_local], axis=1), 'sector'...  218 us
    psum x1, blocking collectives, local(): total = lax.psum(partial_sum, 'term')  78.5 us
    reshape x1, local copies, waits for them, and re-layouts, local(): arrived = arrived.reshape(slots, terms_dev, width, width)  14.6 us
    reshape x1, local copies, waits for them, and re-layouts, local(): packed.reshape(n_sector, capacity, -1)  14.1 us
    all_to_all x1, starting transfers between devices, local(): lax.all_to_all(packed.reshape(n_sector, capacity, -1), 'sector', split_ax...  13.5 us
    dot_general x1, matrix products, local(): jnp.dot(collect, images.reshape(slots, -1), precision=lax.Precision.HIGHE...  10.5 us
    unnamed x10, local copies, waits for them, and re-layouts  9.9 us
    dot_general x1, local copies, waits for them, and re-layouts, local(): jnp.dot(collect, images.reshape(slots, -1), precision=lax.Precision.HIGHE...  8.99 us
  transfers between devices with their start and end apart: 1, of which 0 were waited for; matrix products, arithmetic and copies ran while one was open for 3% of the time, Pallas kernels for 0%

commit v1 on v0

--- a/solution.py
+++ b/solution.py
@@ -56,7 +56,9 @@
         precision=lax.Precision.HIGHEST,
         preferred_element_type=jnp.float32,
     ).reshape(sec_dev, width, width)
-    total = lax.psum(partial_sum, "term")
+    total = partial_sum
+    for hop in (1, 2):
+        total = total + lax.ppermute(total, "term", [(dev, dev ^ hop) for dev in range(4)])
     row_count = width // lax.axis_size("term")
     mine_rows = lax.dynamic_slice_in_dim(total, lax.axis_index("term") * row_count, row_count, 1)
     return mine_rows.astype(jnp.bfloat16)

time: 413 us -> 520 us (1.26)
  waiting for transfers between devices: 0.01 us -> 181 us
  blocking collectives: 297 us -> 218 us
    ppermute x0 -> x2, waiting for transfers between devices: none -> 181 us  [local(): lax.ppermute(total, 'term', [(dev, dev ^ hop) for dev in range(4)])]
    psum x1 -> x0, blocking collectives: 78.5 us -> none  [local(): total = lax.psum(partial_sum, 'term')]
  transfers between devices with their start and end apart: 1 -> 3, of which waited for: 0 -> 2; matrix products, arithmetic and copies ran while one was open for 3% -> 2% of each run, Pallas kernels for 0% -> 0%
where the time goes in v1:
time: 520 us; the launch traced here: 518 us
  blocking collectives  218 us (42%)
  waiting for transfers between devices  181 us (35%)
  local copies, waits for them, and re-layouts  64.3 us (12%)
  matrix products  29.7 us (6%)
  starting transfers between devices  17.5 us (3%)
  other arithmetic  7.32 us (1%)
    all_gather x1, blocking collectives, local(): lax.all_gather(jnp.concatenate([owner_map, left_local], axis=1), 'sector'...  218 us
    ppermute x2, waiting for transfers between devices, local(): lax.ppermute(total, 'term', [(dev, dev ^ hop) for dev in range(4)])  181 us
    reshape x1, local copies, waits for them, and re-layouts, local(): arrived = arrived.reshape(slots, terms_dev, width, width)  14.6 us
    reshape x1, local copies, waits for them, and re-layouts, local(): packed.reshape(n_sector, capacity, -1)  14.1 us
    all_to_all x1, starting transfers between devices, local(): lax.all_to_all(packed.reshape(n_sector, capacity, -1), 'sector', split_ax...  13.5 us
  transfers between devices with their start and end apart: 3, of which 2 were waited for; matrix products, arithmetic and copies ran while one was open for 2% of the time, Pallas kernels for 0%

profile of v1, /device:TPU:1, one launch (start us, length us, event | category | flops | bytes accessed | tf_op | source)
XLA Modules:
  0.0 518.1 jit_solution(12275244872856782721)
XLA Ops:
  0.0 0.9 convert_reduce_fusion.1
  0.9 0.7 multiply_add_fusion
  1.6 0.0 copy-done
  1.6 5.4 %convert_bitcast_fusion = bf16[64,2,128,128]{2,3,1,0:T(8,128)(2,1)} fusion(bf16[2,64,128,128]{3,2,1,0:T(8,128)(2,1)} %param.6, bf16[64,128,128]{2,1,0:T(8,128)(2,1)S(1)} %copy-done), kind=kOutput, calls=%fused_computation.12 | convolution fusion | flops 538968064 | bytes 10485760 | tf_op jit(solution)/shard_map/sij,tsjk->stik/dot_general | solution.py:38
  7.0 6.3 %copy.23 = bf16[64,2,128,128]{3,2,1,0:T(8,128)(2,1)} copy(bf16[64,2,128,128]{2,3,1,0:T(8,128)(2,1)} %convert_bitcast_fusion) | data formatting | bytes 8388608 | tf_op jit(solution)/shard_map/convert_element_type | solution.py:40
  13.4 8.8 %convolution_convert_fusion = bf16[128,32768]{1,0:T(8,128)(2,1)} fusion(bf16[8,8,256,128]{3,2,1,0:T(8,128)(2,1)} %bitcast.41, s32[64]{0:T(128)S(1)} %multiply_add_fusion), kind=kOutput, calls=%fused_computation.1 | convolution fusion | flops 541073408 | bytes 12583168 | tf_op jit(solution)/shard_map/dot_general | solution.py:41
  22.1 14.1 %reshape.90 = bf16[64,2,32768]{2,1,0:T(2,128)(2,1)} reshape(bf16[128,32768]{1,0:T(8,128)(2,1)} %convolution_convert_fusion) | data formatting | bytes 16777216 | tf_op jit(solution)/shard_map/reshape | solution.py:45
  36.3 13.5 %all-to-all-start = ((bf16[64,2,32768]{2,1,0:T(2,128)(2,1)}), bf16[64,2,32768]{2,1,0:T(2,128)(2,1)}, u32[]{:S(2)}, u32[]{:S(2)}) async-start(bf16[64,2,32768]{2,1,0:T(2,128)(2,1)} %reshape.90), calls=%async_computation | async-start | bytes 16777216 | tf_op jit(solution)/shard_map/all_to_all | solution.py:44
  49.8 218.2 %all-gather = s32[64,64,2]{1,2,0:T(2,128)S(1)} all-gather(s32[1,64,2]{1,2,0:T(2,128)S(1)} %add_bitcast_fusion), channel_id=1, replica_groups=mesh['term'=4,'sector'=64] {'sector'}, dimensions={0}, use_global_device_ids=true | all-gather | bytes 33280 | tf_op jit(solution)/shard_map/all_gather | solution.py:28
  268.0 0.1 reshape.102
  268.1 0.1 slice_reduce_fusion
  268.2 0.1 reshape_squeeze.3
  268.3 0.1 add.70
  268.4 0.9 convert_reduce_fusion
  269.3 0.1 select_reduce_fusion
  269.4 0.1 copy.20
  269.5 0.1 sub.7
  269.7 0.1 copy.21
  269.8 0.1 min.18
  269.9 8.6 %gather_fusion = bf16[128,2,128,128]{3,2,1,0:T(8,128)(2,1)} fusion(bf16[2,64,128,128]{3,2,1,0:T(8,128)(2,1)} %param.7, s32[1024]{0:T(1024)S(1)} %pad_clamp_fusion), kind=kCustom, calls=%fused_computation | custom fusion | bytes 16777728 | tf_op jit(solution)/shard_map/jit(_take)/gather | solution.py:48
  278.5 14.6 %reshape.91 = bf16[128,2,128,128]{3,2,1,0:T(8,128)(2,1)} reshape(bf16[64,2,32768]{2,1,0:T(2,128)(2,1)} %all-to-all-done) | data formatting | bytes 16777216 | tf_op jit(solution)/shard_map/reshape | solution.py:47
  293.1 8.2 %fusion = f32[128,128,128,1]{2,1,3,0:T(8,128)S(1)} fusion(bf16[128,2,128,128]{3,2,1,0:T(8,128)(2,1)} %reshape.91, bf16[128,2,128,128]{3,2,1,0:T(8,128)(2,1)} %gather_fusion, pred[128]{0:T(512)(128)(4,1)S(1)} %compare_and_fusion), kind=kOutput, calls=%fused_computation.3 | convolution fusion | flops 1077936128 | bytes 25165952 | tf_op jit(solution)/shard_map/tnij,ntjk->nik/dot_general | solution.py:49
  301.3 9.8 %copy.41 = f32[16,8,128,128]{3,1,2,0:T(8,128)} copy(f32[16,8,128,128]{3,2,1,0:T(8,128)S(1)} %bitcast.38) | data formatting | bytes 16777216
  311.1 9.0 %copy.24 = f32[16384,128]{1,0:T(8,128)} copy(f32[16384,128]{0,1:T(8,128)} %bitcast.40) | data formatting | bytes 16777216 | tf_op jit(solution)/shard_map/dot_general | solution.py:53
  320.1 7.4 %fusion.16 = f32[64,128,128]{2,0,1:T(8,128)S(1)} fusion(f32[128,128,128]{2,1,0:T(8,128)} %bitcast.39, s32[128]{0:T(128)S(1)} %sub.7), kind=kOutput, calls=%fused_computation.26 | convolution fusion | flops 1610620928 | bytes 12583424 | tf_op jit(solution)/shard_map/dot_general | solution.py:53
  327.4 1.3 collective-permute-start
  328.7 90.7 %collective-permute-done = f32[64,128,128]{2,0,1:T(8,128)S(1)} collective-permute-done((f32[64,128,128]{2,0,1:T(8,128)S(1)}, f32[64,128,128]{2,0,1:T(8,128)S(1)}, u32[]{:S(2)}, u32[]{:S(2)}) %collective-permute-start) | collective-permute-done | bytes 4194336 | tf_op jit(solution)/shard_map/ppermute | solution.py:61
  419.5 2.9 add.76
  422.4 2.7 collective-permute-start.1
  425.1 90.2 %collective-permute-done.1 = f32[64,128,128]{2,0,1:T(8,128)} collective-permute-done((f32[64,128,128]{2,0,1:T(8,128)}, f32[64,128,128]{2,0,1:T(8,128)}, u32[]{:S(2)}, u32[]{:S(2)}) %collective-permute-start.1) | collective-permute-done | bytes 4194336 | tf_op jit(solution)/shard_map/ppermute | solution.py:61
  515.3 1.7 fusion.12
  517.0 1.1 copy.25
  (16 shorter events, 0.1 us)
Async XLA Ops:
  0.0 1.6 copy-start
  36.3 13.5 %copy-start.2 = (s32[64,1]{0,1:T(1,128)S(1)}, s32[64,1]{0,1:T(1,128)}, u32[]{:S(2)}) copy-start(s32[64,1]{0,1:T(1,128)} %param.8) | copy-start | bytes 772
  36.3 13.5 %copy-start.3 = (s32[64,1]{0,1:T(1,128)S(1)}, s32[64,1]{0,1:T(1,128)}, u32[]{:S(2)}) copy-start(s32[64,1]{0,1:T(1,128)} %param.9) | copy-start | bytes 772
  36.3 242.2 %all-to-all-start = ((bf16[64,2,32768]{2,1,0:T(2,128)(2,1)}), bf16[64,2,32768]{2,1,0:T(2,128)(2,1)}, u32[]{:S(2)}, u32[]{:S(2)}) async-start(bf16[64,2,32768]{2,1,0:T(2,128)(2,1)} %reshape.90), calls=%async_computation | async-start | bytes 16777216 | tf_op jit(solution)/shard_map/all_to_all | solution.py:44
  327.4 92.0 %collective-permute-start = (f32[64,128,128]{2,0,1:T(8,128)S(1)}, f32[64,128,128]{2,0,1:T(8,128)S(1)}, u32[]{:S(2)}, u32[]{:S(2)}) collective-permute-start(f32[64,128,128]{2,0,1:T(8,128)S(1)} %fusion.16), channel_id=1, source_target_pairs={{0,64},{64,0},{128,192},{192,128},{1,65},{65,1},{129,193},{193,129... | collective-permute-start | bytes 12582920 | tf_op jit(solution)/shard_map/ppermute | solution.py:61
  419.5 98.7 %copy-start.1 = (bf16[64,128,128]{2,1,0:T(8,128)(2,1)S(1)}, bf16[64,128,128]{2,1,0:T(8,128)(2,1)}, u32[]{:S(2)}) copy-start(bf16[64,128,128]{2,1,0:T(8,128)(2,1)} %param.5) | copy-start | bytes 6291460
  422.4 92.9 %collective-permute-start.1 = (f32[64,128,128]{2,0,1:T(8,128)}, f32[64,128,128]{2,0,1:T(8,128)}, u32[]{:S(2)}, u32[]{:S(2)}) collective-permute-start(f32[64,128,128]{2,0,1:T(8,128)} %add.76), channel_id=1, source_target_pairs={{0,128},{64,192},{128,0},{192,64},{1,129},{65,193},{129,1},{193,65... | collective-permute-start | bytes 12582920 | tf_op jit(solution)/shard_map/ppermute | solution.py:61
